TPU v7x, 256 devices: a whole 4x4x8 slice. The times are simulated.
256 devices in a mesh: row: 32 (over z, x), col: 4 (over y), rep: 2 (over core).
Axes of the slice: x: 4, y: 4, z: 8, core: 2. Of those that a mesh axis runs over, the one named last changes fastest.
Arguments:
- amplitudes: bfloat16 [32768, 8192], P('row', ('rep', 'col')), may hold values from -6 to 6
- integrals: bfloat16 [8192, 4096], P(('rep', 'row'), 'col'), may hold values from -0.1875 to 0.1875
- tile_mask: int32 [64, 32], replicated, may hold values from 0 to 1
- k_irrep: int32 [64], replicated, may hold values from 0 to 3
- n_irrep: int32 [32], replicated, may hold values from 0 to 3
- stored_tile: int32 [64], replicated, may hold values from 0 to 63, as said below
Outputs:
- ladder: bfloat16 [32768, 4096], P('row', ('col', 'rep'))
Inputs may be any that keep to these rules, and one draw needn't show every extreme that they name: `stored_tile`: for each q, slots q * 32 to (q + 1) * 32 - 1 hold a permutation of the tiles q * 32 to (q + 1) * 32 - 1.
All inputs are finite; a program needn't handle non-finite values.
Results may differ from a plain program's by a relative error of at most 0.001.
Values may be sent and summed in bfloat16 or wider, within the bound.
No kernel may reach another device: no remote copies, remote signals or barrier semaphores. Data moves between devices by JAX's collectives and lax.ppermute only.
A program may use at most 128 MiB of HBM per device.

v0:
```python
import jax
import jax.numpy as jnp
from jax import lax
from jax.sharding import PartitionSpec as P

TS = 128


def on_device(amplitudes, integrals, tile_mask, k_irrep, n_irrep, stored_tile):
    slab = lax.axis_index("rep")
    column = lax.axis_index("col")
    ncol = integrals.shape[1]
    tiles_col = ncol // TS
    n_labels = lax.dynamic_slice_in_dim(n_irrep, column * tiles_col, tiles_col)
    mask_cols = lax.dynamic_slice_in_dim(tile_mask, column * tiles_col, tiles_col, 1)
    stored_rows = integrals.shape[0]
    kq = stored_rows * lax.axis_size("row")
    slab_tiles = kq // TS
    slots = lax.dynamic_slice_in_dim(stored_tile, slab * slab_tiles, slab_tiles)
    gathered = lax.all_gather(integrals, "row", axis=0, tiled=True)
    same = jnp.take(k_irrep, slots)[:, None] == n_labels[None, :]
    occupied = jnp.take(mask_cols, slots, axis=0) == 1
    weights = jnp.logical_and(same, occupied).astype(jnp.bfloat16)
    shaped = gathered.reshape(slab_tiles, TS, tiles_col, TS) * weights[:, None, :, None]
    masked = shaped.reshape(kq, ncol)
    amp_slab = lax.all_gather(amplitudes, "col", axis=1, tiled=True)
    mrow = amp_slab.shape[0]
    local_ids = slots - slab * slab_tiles
    ordered = jnp.take(amp_slab.reshape(mrow, slab_tiles, TS), local_ids, axis=1).reshape(mrow, kq)
    partial_value = jnp.dot(ordered, masked, preferred_element_type=jnp.float32)
    return lax.psum_scatter(partial_value, "rep", scatter_dimension=1, tiled=True).astype(
        jnp.bfloat16
    )


def solution(mesh):
    placed = (P("row", ("rep", "col")), P(("rep", "row"), "col"), P(), P(), P(), P())
    return jax.shard_map(
        on_device, mesh=mesh, in_specs=placed, out_specs=P("row", ("col", "rep")), check_vma=False
    )
```

profile of v0, /device:TPU:1, one launch (start us, length us, event | category | flops | bytes accessed | tf_op | source)
XLA Modules:
  0.0 242.3 jit_solution(16062950526228524270)
XLA Ops:
  6.5 0.0 copy-start
  6.5 0.0 all-gather.3.cloned.1.call-start
  6.5 3.9 %copy.13 = bf16[1024,1024]{0,1:T(8,128)(2,1)} copy(bf16[1024,1024]{1,0:T(8,128)(2,1)} %param.6) | data formatting | bytes 4194304 | tf_op args[0]
  10.5 0.0 all-gather.3.cloned.1.call-update
  10.5 0.0 all-gather.5.cloned.1.call-start
  10.6 0.7 all-gather.5.cloned.1.call-update
  11.3 0.0 reduce-scatter.2.cloned.1.call-start
  11.3 0.7 dynamic_slice.10
  12.0 0.0 copy-done
  12.0 0.1 copy.19
  12.1 0.7 compare_and_fusion
  12.9 1.4 gather_fusion.1
  14.2 0.6 gather_fusion.2
  14.8 0.1 copy.17
  14.9 0.1 fusion.3
  15.0 0.1 copy.18
  15.1 0.1 broadcast_bitcast_fusion
  15.1 84.8 %all-gather.3.cloned.1.call-done = bf16[1024,4096]{0,1:T(8,128)(2,1)} async-done(((bf16[1024,1024]{0,1:T(8,128)(2,1)}), bf16[1024,4096]{0,1:T(8,128)(2,1)}) %all-gather.3.cloned.1.call-update) | async-done | bytes 8388624 | tf_op jit(solution)/shard_map/all_gather | solution.py:26
  99.9 12.0 %copy.14 = bf16[1024,32,128]{2,0,1:T(8,128)(2,1)} copy(bf16[1024,32,128]{0,2,1:T(8,128)(2,1)} %bitcast.14) | data formatting | bytes 16777216 | tf_op jit(solution)/shard_map/reshape | solution.py:29
  111.9 8.4 %gather_fusion = bf16[32,1024,128]{2,1,0:T(8,128)(2,1)} fusion(bf16[1024,32,128]{2,0,1:T(8,128)(2,1)} %copy.14, s32[1024]{0:T(1024)S(1)} %pad_clamp_fusion.1), kind=kCustom, calls=%fused_computation | custom fusion | bytes 16777344 | tf_op jit(solution)/shard_map/jit(_take)/gather | solution.py:29
  120.3 12.0 %copy.15 = bf16[1024,32,128]{0,2,1:T(8,128)(2,1)} copy(bf16[1024,32,128]{2,0,1:T(8,128)(2,1)} %bitcast.12) | data formatting | bytes 16777216 | tf_op jit(solution)/shard_map/jit(_take)/gather | solution.py:29
  132.3 7.3 %bitcast_select_fusion = bf16[1024,4096]{0,1:T(8,128)(2,1)} fusion(bf16[1024,32,128]{0,2,1:T(8,128)(2,1)} %copy.15, pred[4096]{0:T(1024)(128)(4,1)S(1)} %broadcast_bitcast_fusion), kind=kLoop, calls=%fused_computation.6 | loop fusion | flops 4194304 | bytes 16781312 | tf_op jit(solution)/shard_map/jit(_take)/select_n | solution.py:29
  139.6 61.2 %all-gather.5.cloned.1.call-done = bf16[4096,1024]{1,0:T(8,128)(2,1)} async-done(((bf16[128,1024]{1,0:T(8,128)(2,1)}), bf16[4096,1024]{1,0:T(8,128)(2,1)}) %all-gather.5.cloned.1.call-update) | async-done | bytes 8388624 | tf_op jit(solution)/shard_map/all_gather | solution.py:20
  200.8 0.0 copy-start.2
  200.8 1.1 mul.21
  201.9 2.2 copy-done.2
  204.2 0.0 copy-start.1
  204.2 13.0 %fusion = f32[1024,1024]{1,0:T(8,128)} fusion(bf16[1024,4096]{0,1:T(8,128)(2,1)S(1)} %copy-done.2, bf16[4096,1024]{1,0:T(8,128)(2,1)} %all-gather.5.cloned.1.call-done, bf16[512,8,8,128]{3,2,1,0:T(8,128)(2,1)S(1)} %bitcast.13), kind=kOutput, calls=%fused_computation.4 | convolution fusion | flops 8594128896 | bytes 29360128 | tf_op jit(solution)/shard_map/dot_general | solution.py:30
  217.1 0.0 reduce-scatter.2.cloned.1.call-update
  217.1 16.0 %reduce-scatter.2.cloned.1.call-done = f32[1024,512]{1,0:T(8,128)} async-done(((f32[1024,1024]{1,0:T(8,128)}), f32[1024,512]{1,0:T(8,128)}) %reduce-scatter.2.cloned.1.call-update) | async-done | bytes 2097168 | tf_op jit(solution)/shard_map/reduce_scatter | solution.py:31
  233.1 2.7 %convert_element_type.11 = bf16[1024,512]{1,0:T(8,128)(2,1)} convert(f32[1024,512]{1,0:T(8,128)} %reduce-scatter.2.cloned.1.call-done) | non-fusion elementwise | flops 524288 | bytes 3145728 | tf_op jit(solution)/shard_map/convert_element_type | solution.py:31
  235.8 0.0 copy-done.1
  (4 shorter events, 0.0 us)
Async XLA Ops:
  6.5 5.5 %copy-start = (s32[64,32]{0,1:T(8,128)S(1)}, s32[64,32]{0,1:T(8,128)}, u32[]{:S(2)}) copy-start(s32[64,32]{0,1:T(8,128)} %param.8) | copy-start | bytes 24580
  6.5 93.4 %all-gather.3.cloned.1.call-start = ((), (), s32[]{:S(2)}) async-start(), calls=%async_computation.1 | async-start | bytes 10485760 | tf_op jit(solution)/shard_map/all_gather | solution.py:26
  10.5 190.3 %all-gather.5.cloned.1.call-start = ((), (), s32[]{:S(2)}) async-start(), calls=%async_computation.2 | async-start | bytes 8650752 | tf_op jit(solution)/shard_map/all_gather | solution.py:20
  11.3 221.9 %reduce-scatter.2.cloned.1.call-start = ((), (), s32[]{:S(2)}) async-start(), calls=%async_computation.3 | async-start | bytes 6291456 | tf_op jit(solution)/shard_map/reduce_scatter | solution.py:31
  200.8 3.4 %copy-start.2 = (bf16[1024,4096]{0,1:T(8,128)(2,1)S(1)}, bf16[1024,4096]{0,1:T(8,128)(2,1)}, u32[]{:S(2)}) copy-start(bf16[1024,4096]{0,1:T(8,128)(2,1)} %bitcast_select_fusion) | copy-start | bytes 25165828
  204.2 31.7 %copy-start.1 = (s32[64,32]{0,1:T(8,128)S(1)}, s32[64,32]{0,1:T(8,128)}, u32[]{:S(2)}) copy-start(s32[64,32]{0,1:T(8,128)} %param.8) | copy-start | bytes 24580
Sparse Core Ops, SparseCore 0:
  10.6 89.2 all-gather.2
  102.5 98.2 all-gather.4
  217.3 15.8 reduce-scatter.1
where the time goes:
time: 243 us; the launch traced here: 242 us
  waiting for transfers between devices  163 us (67%)
  local copies, waits for them, and re-layouts  42.7 us (18%)
  between operations  13.1 us (5%)
  matrix products  13 us (5%)
  other arithmetic  10.8 us (4%)
    all_gather x1, waiting for transfers between devices, on_device(): amp_slab = lax.all_gather(amplitudes, 'col', axis=1, tiled=True)  84.8 us
    all_gather x1, waiting for transfers between devices, on_device(): gathered = lax.all_gather(integrals, 'row', axis=0, tiled=True)  61.2 us
    gather x2, local copies, waits for them, and re-layouts, on_device(): jnp.take(amp_slab.reshape(mrow, slab_tiles, TS), local_ids, axis=1)  20.4 us
    reduce_scatter x1, waiting for transfers between devices, on_device(): lax.psum_scatter(partial_value, 'rep', scatter_dimension=1, tiled=True)  16 us
    dot_general x1, matrix products, on_device(): partial_value = jnp.dot(ordered, masked, preferred_element_type=jnp.float32)  13 us
    reshape x1, local copies, waits for them, and re-layouts, on_device(): amp_slab.reshape(mrow, slab_tiles, TS)  12 us
    select_n x1, other arithmetic, on_device(): jnp.take(amp_slab.reshape(mrow, slab_tiles, TS), local_ids, axis=1)  7.27 us
    unnamed x8, local copies, waits for them, and re-layouts  6.26 us
  transfers between devices with their start and end apart: 3, of which 3 were waited for; matrix products, arithmetic and copies ran while one was open for 18% of the time, Pallas kernels for 0%

commit v1 on v0

--- a/solution.py
+++ b/solution.py
@@ -23,7 +23,12 @@
     weights = jnp.logical_and(same, occupied).astype(jnp.bfloat16)
     shaped = gathered.reshape(slab_tiles, TS, tiles_col, TS) * weights[:, None, :, None]
     masked = shaped.reshape(kq, ncol)
-    amp_slab = lax.all_gather(amplitudes, "col", axis=1, tiled=True)
+    amp_slab = jnp.concatenate(
+        lax.all_to_all(
+            jnp.stack([amplitudes for _ in range(lax.axis_size("col"))], axis=0), "col", 0, 0
+        ),
+        axis=1,
+    )
     mrow = amp_slab.shape[0]
     local_ids = slots - slab * slab_tiles
     ordered = jnp.take(amp_slab.reshape(mrow, slab_tiles, TS), local_ids, axis=1).reshape(mrow, kq)

time: 243 us -> 201 us (0.83)
  waiting for transfers between devices: 163 us -> 113 us
  starting transfers between devices: 0.08 us -> 5.84 us
    all_to_all x0 -> x1, waiting for transfers between devices: none -> 90.2 us  [on_device(): lax.all_to_all(jnp.stack([amplitudes for _ in range(lax.axis_size('col'))...]
    all_gather x1 -> x0, waiting for transfers between devices: 84.8 us -> none  [on_device(): amp_slab = lax.all_gather(amplitudes, 'col', axis=1, tiled=True)]
    all_gather x1, waiting for transfers between devices: 61.2 us -> 0.01 us  [on_device(): gathered = lax.all_gather(integrals, 'row', axis=0, tiled=True)]
    another operation x0 -> x2, local copies, waits for them, and re-layouts: none -> 16.3 us  [the longest x1 12 us: on_device(): amp_slab.reshape(mrow, slab_tiles, TS)]
    reshape x1 -> x0, local copies, waits for them, and re-layouts: 12 us -> none  [on_device(): amp_slab.reshape(mrow, slab_tiles, TS)]
    reduce_scatter x1, waiting for transfers between devices: 16 us -> 21.9 us  [on_device(): lax.psum_scatter(partial_value, 'rep', scatter_dimension=1, tiled=True)]
    all_to_all x0 -> x1, starting transfers between devices: none -> 5.8 us  [on_device(): lax.all_to_all(jnp.stack([amplitudes for _ in range(lax.axis_size('col'))...]
    unnamed x8 -> x14, local copies, waits for them, and re-layouts: 6.26 us -> 5.2 us
  transfers between devices with their start and end apart: 3 -> 3, of which waited for: 3 -> 2; matrix products, arithmetic and copies ran while one was open for 18% -> 24% of each run, Pallas kernels for 0% -> 0%
where the time goes in v1:
time: 201 us; the launch traced here: 200 us
  waiting for transfers between devices  113 us (56%)
  local copies, waits for them, and re-layouts  44.6 us (22%)
  between operations  13.5 us (7%)
  matrix products  12.9 us (6%)
  other arithmetic  10.1 us (5%)
  starting transfers between devices  5.84 us (3%)
    all_to_all x1, waiting for transfers between devices, on_device(): lax.all_to_all(jnp.stack([amplitudes for _ in range(lax.axis_size('col'))...  90.2 us
    reduce_scatter x1, waiting for transfers between devices, on_device(): lax.psum_scatter(partial_value, 'rep', scatter_dimension=1, tiled=True)  21.9 us
    gather x2, local copies, waits for them, and re-layouts, on_device(): jnp.take(amp_slab.reshape(mrow, slab_tiles, TS), local_ids, axis=1)  20.4 us
    dot_general x1, matrix products, on_device(): partial_value = jnp.dot(ordered, masked, preferred_element_type=jnp.float32)  12.9 us
    another operation x1, local copies, waits for them, and re-layouts, on_device(): amp_slab.reshape(mrow, slab_tiles, TS)  12 us
    select_n x1, other arithmetic, on_device(): jnp.take(amp_slab.reshape(mrow, slab_tiles, TS), local_ids, axis=1)  7.25 us
    all_to_all x1, starting transfers between devices, on_device(): lax.all_to_all(jnp.stack([amplitudes for _ in range(lax.axis_size('col'))...  5.8 us
    unnamed x14, local copies, waits for them, and re-layouts  5.2 us
  transfers between devices with their start and end apart: 3, of which 2 were waited for; matrix products, arithmetic and copies ran while one was open for 24% of the time, Pallas kernels for 0%

profile of v1, /device:TPU:1, one launch (start us, length us, event | category | flops | bytes accessed | tf_op | source)
XLA Modules:
  0.0 199.8 jit_solution(5010650711979478620)
XLA Ops:
  6.5 0.0 copy-start
  6.5 0.0 all-gather.2.cloned.1.call-start
  6.5 0.7 all-gather.2.cloned.1.call-update
  7.3 2.9 %copy.15 = bf16[1024,1024]{0,1:T(8,128)(2,1)S(1)} copy(bf16[1024,1024]{1,0:T(8,128)(2,1)} %param.6) | data formatting | bytes 4194304 | tf_op args[0]
  10.1 4.3 %stack.2 = bf16[4,1024,1024]{1,2,0:T(8,128)(2,1)} broadcast(bf16[1024,1024]{0,1:T(8,128)(2,1)S(1)} %copy.15), dimensions={1,2} | broadcast | bytes 10485760 | tf_op jit(solution)/shard_map/stack | solution.py:28
  14.4 0.0 copy-start.5
  14.4 0.0 copy-start.4
  14.5 0.0 copy-start.2
  14.5 5.8 %all-to-all-start = ((bf16[4,1024,1024]{1,2,0:T(8,128)(2,1)}), bf16[4,1024,1024]{1,2,0:T(8,128)(2,1)}, u32[]{:S(2)}, u32[]{:S(2)}) async-start(bf16[4,1024,1024]{1,2,0:T(8,128)(2,1)} %stack.2), calls=%async_computation | async-start | bytes 16777216 | tf_op jit(solution)/shard_map/all_to_all | solution.py:27
  20.3 0.0 reduce-scatter.2.cloned.1.call-start
  20.3 0.0 copy-done.5
  20.3 0.1 dynamic_slice.10
  20.4 0.0 copy-done
  20.4 0.1 copy.21
  20.5 0.0 copy-done.4
  20.5 0.1 compare_and_fusion
  20.6 0.0 copy-done.2
  20.6 0.7 gather_fusion.1
  21.3 0.6 gather_fusion.2
  21.9 0.1 copy.19
  22.0 0.1 fusion.3
  22.0 0.1 copy.20
  22.1 0.1 broadcast_bitcast_fusion
  22.2 90.2 %all-to-all-done = bf16[4,1024,1024]{1,2,0:T(8,128)(2,1)} async-done(((bf16[4,1024,1024]{1,2,0:T(8,128)(2,1)}), bf16[4,1024,1024]{1,2,0:T(8,128)(2,1)}, u32[]{:S(2)}, u32[]{:S(2)}) %all-to-all-start) | async-done | bytes 8388640 | tf_op jit(solution)/shard_map/all_to_all | solution.py:27
  112.4 12.0 %copy.16 = bf16[1024,32,128]{2,0,1:T(8,128)(2,1)} copy(bf16[1024,32,128]{0,2,1:T(8,128)(2,1)} %bitcast.2) | data formatting | bytes 16777216 | tf_op jit(solution)/shard_map/reshape;reshape | solution.py:34
  124.4 8.4 %gather_fusion = bf16[32,1024,128]{2,1,0:T(8,128)(2,1)} fusion(bf16[1024,32,128]{2,0,1:T(8,128)(2,1)} %copy.16, s32[1024]{0:T(1024)S(1)} %pad_clamp_fusion.1), kind=kCustom, calls=%fused_computation | custom fusion | bytes 16777344 | tf_op jit(solution)/shard_map/jit(_take)/gather | solution.py:34
  132.8 12.0 %copy.17 = bf16[1024,32,128]{0,2,1:T(8,128)(2,1)} copy(bf16[1024,32,128]{2,0,1:T(8,128)(2,1)} %bitcast.14) | data formatting | bytes 16777216 | tf_op jit(solution)/shard_map/jit(_take)/gather | solution.py:34
  144.8 7.2 %bitcast_select_fusion = bf16[1024,4096]{0,1:T(8,128)(2,1)} fusion(bf16[1024,32,128]{0,2,1:T(8,128)(2,1)} %copy.17, pred[4096]{0:T(1024)(128)(4,1)S(1)} %broadcast_bitcast_fusion), kind=kLoop, calls=%fused_computation.6 | loop fusion | flops 4194304 | bytes 16781312 | tf_op jit(solution)/shard_map/jit(_take)/select_n | solution.py:34
  152.0 0.0 all-gather.2.cloned.1.call-done
  152.0 0.0 copy-start.3
  152.0 1.1 mul.21
  153.2 2.2 %copy-done.3 = bf16[1024,4096]{0,1:T(8,128)(2,1)S(1)} copy-done((bf16[1024,4096]{0,1:T(8,128)(2,1)S(1)}, bf16[1024,4096]{0,1:T(8,128)(2,1)}, u32[]{:S(2)}) %copy-start.3) | copy-done | bytes 8388632
  155.4 0.0 copy-start.1
  155.4 12.9 %fusion = f32[1024,1024]{1,0:T(8,128)} fusion(bf16[1024,4096]{0,1:T(8,128)(2,1)S(1)} %copy-done.3, bf16[4096,1024]{1,0:T(8,128)(2,1)} %all-gather.2.cloned.1.call-done, bf16[512,8,8,128]{3,2,1,0:T(8,128)(2,1)S(1)} %bitcast.15), kind=kOutput, calls=%fused_computation.4 | convolution fusion | flops 8594128896 | bytes 29360128 | tf_op jit(solution)/shard_map/dot_general | solution.py:35
  168.3 0.0 reduce-scatter.2.cloned.1.call-update
  168.4 21.9 %reduce-scatter.2.cloned.1.call-done = f32[1024,512]{1,0:T(8,128)} async-done(((f32[1024,1024]{1,0:T(8,128)}), f32[1024,512]{1,0:T(8,128)}) %reduce-scatter.2.cloned.1.call-update) | async-done | bytes 2097168 | tf_op jit(solution)/shard_map/reduce_scatter | solution.py:36
  190.2 2.7 %convert_element_type.11 = bf16[1024,512]{1,0:T(8,128)(2,1)} convert(f32[1024,512]{1,0:T(8,128)} %reduce-scatter.2.cloned.1.call-done) | non-fusion elementwise | flops 524288 | bytes 3145728 | tf_op jit(solution)/shard_map/convert_element_type | solution.py:36
  192.9 0.0 copy-done.1
  (4 shorter events, 0.0 us)
Async XLA Ops:
  6.5 13.9 %copy-start = (s32[64,32]{0,1:T(8,128)S(1)}, s32[64,32]{0,1:T(8,128)}, u32[]{:S(2)}) copy-start(s32[64,32]{0,1:T(8,128)} %param.8) | copy-start | bytes 24580
  6.5 145.5 %all-gather.2.cloned.1.call-start = ((), (), s32[]{:S(2)}) async-start(), calls=%async_computation.2 | async-start | bytes 8650752 | tf_op jit(solution)/shard_map/all_gather | solution.py:20
  14.4 5.9 %copy-start.5 = (s32[32]{0:T(128)S(1)}, s32[32]{0:T(128)}, u32[]{:S(2)}) copy-start(s32[32]{0:T(128)} %param.10) | copy-start | bytes 388
  14.4 6.0 %copy-start.4 = (s32[64]{0:T(128)S(1)}, s32[64]{0:T(128)}, u32[]{:S(2)}) copy-start(s32[64]{0:T(128)} %param.11) | copy-start | bytes 772
  14.5 6.1 %copy-start.2 = (s32[64]{0:T(128)S(1)}, s32[64]{0:T(128)}, u32[]{:S(2)}) copy-start(s32[64]{0:T(128)} %param.9) | copy-start | bytes 772
  14.5 97.9 %all-to-all-start = ((bf16[4,1024,1024]{1,2,0:T(8,128)(2,1)}), bf16[4,1024,1024]{1,2,0:T(8,128)(2,1)}, u32[]{:S(2)}, u32[]{:S(2)}) async-start(bf16[4,1024,1024]{1,2,0:T(8,128)(2,1)} %stack.2), calls=%async_computation | async-start | bytes 16777216 | tf_op jit(solution)/shard_map/all_to_all | solution.py:27
  20.3 170.0 %reduce-scatter.2.cloned.1.call-start = ((), (), s32[]{:S(2)}) async-start(), calls=%async_computation.3 | async-start | bytes 6291456 | tf_op jit(solution)/shard_map/reduce_scatter | solution.py:36
  152.0 3.4 %copy-start.3 = (bf16[1024,4096]{0,1:T(8,128)(2,1)S(1)}, bf16[1024,4096]{0,1:T(8,128)(2,1)}, u32[]{:S(2)}) copy-start(bf16[1024,4096]{0,1:T(8,128)(2,1)} %bitcast_select_fusion) | copy-start | bytes 25165828
  155.4 37.5 %copy-start.1 = (s32[64,32]{0,1:T(8,128)S(1)}, s32[64,32]{0,1:T(8,128)}, u32[]{:S(2)}) copy-start(s32[64,32]{0,1:T(8,128)} %param.8) | copy-start | bytes 24580
Sparse Core Ops, SparseCore 0:
  9.9 100.8 all-gather.1
  168.5 21.6 reduce-scatter.1
